TPU v7x, 128 devices: a whole 4x4x4 slice. The times are simulated.
128 devices in a mesh: grid: 32 (over y, x, z_lo), ipts: 4 (over z_hi, core).
Axes of the slice: x: 4, y: 4, z: 4 (z_hi: 2, z_lo: 2; z = z_hi * 2 + z_lo), core: 2. Of those that a mesh axis runs over, the one named last changes fastest.
Arguments:
- orbitals: bfloat16 [65536, 1024], P(('grid', 'ipts')), may hold values from -1.1953125 to 1.1953125
- targets: bfloat16 [65536, 256], P(('grid', 'ipts')), may hold values from -6 to 6
- points: int32 [4, 4096], P('ipts', 'grid'), may hold values from 0 to 65535, as said below
- potential: bfloat16 [65536, 16384], P('grid', 'ipts'), may hold values from -0.046875 to 0.046875
Outputs:
- exchanged: bfloat16 [65536, 256], P(('grid', 'ipts'))
Inputs may be any that keep to these rules, and one draw needn't show every extreme that they name: Indices are distinct over all groups; each row of points rises strictly, and its entries k * 128 to (k + 1) * 128 - 1 lie in grid rows k * 2048 to (k + 1) * 2048 - 1.
All inputs are finite; a program needn't handle non-finite values.
Results may differ from a plain program's by a relative error of at most 0.0049.
Values may be sent and summed in bfloat16 or wider, within the bound.
No kernel may reach another device: no remote copies, remote signals or barrier semaphores. Data moves between devices by JAX's collectives and lax.ppermute only.
A program may use at most 128 MiB of HBM per device.

v0:
```python
import jax
import jax.numpy as jnp
from jax import lax
from jax.sharding import Mesh
from jax.sharding import PartitionSpec as P

IPTS = ("ipts_0", "ipts_1")
GRID_IPTS = ("grid", "ipts_0", "ipts_1")


def in_order(pieces, dim):
    dims = list(pieces.shape[1:])
    dims[dim] *= pieces.shape[0]
    return jnp.moveaxis(pieces, 0, dim).reshape(dims)


def gather_in_order(value, axes, turns):
    pieces = value
    for k in turns:
        pieces = lax.all_gather(pieces, axes[k])
    done = turns[::-1]
    back = [done.index(k) for k in range(len(axes))]
    pieces = pieces.transpose(*back, *range(len(axes), pieces.ndim))
    return pieces.reshape(-1, *value.shape)


def whole_of(value, axes, turns, dim):
    return in_order(gather_in_order(value, axes, turns), dim)


def split_up(value, dim, length):
    before, after = (value.shape[:dim], value.shape[dim + 1 :])
    return jnp.moveaxis(value.reshape(*before, length, -1, *after), dim, 0)


def sum_at_owner(value, axis, dim):
    pieces = split_up(value, dim, lax.axis_size(axis))
    arrived = lax.all_to_all(pieces, axis, split_axis=0, concat_axis=0, tiled=True)
    return arrived.astype(jnp.float32).sum(axis=0)


def sent_together(arrays, axis, dim, along):
    both = jnp.concatenate(arrays, axis=along)
    whole, at, finished = (lax.all_gather(both, axis, axis=dim, tiled=True), 0, [])
    for a in arrays:
        finished.append(lax.slice_in_dim(whole, at, at + a.shape[along], axis=along))
        at += a.shape[along]
    return tuple(finished)


def summed_on_arrival(value, axis, dim):
    length = lax.axis_size(axis)
    pieces = lax.all_to_all(split_up(value, dim, length), axis, 0, 0, tiled=True)
    return jnp.sum(pieces, axis=0)


def local(orbitals, targets, points, potential):
    groups = lax.axis_size(IPTS)
    own_rows = orbitals.shape[0]
    slab_length = own_rows * groups
    slab_start = lax.axis_index("grid") * slab_length
    whole_slab = lax.all_gather(orbitals, IPTS, axis=0, tiled=True)
    every_group = whole_of(points, IPTS, (0, 1), 0)
    orbital_values = jnp.take(whole_slab, points[0] - slab_start, axis=0)
    offset = every_group - (slab_start + lax.axis_index(IPTS) * own_rows)
    inside = (offset >= 0) & (offset < own_rows)
    clipped = jnp.clip(offset, 0, own_rows - 1)
    picked = jnp.take(targets, clipped, axis=0) * inside[:, :, None].astype(targets.dtype)
    summed = sum_at_owner(picked, IPTS, 0)
    target_values = summed[0].astype(jnp.bfloat16)
    orbital_piece, target_piece = sent_together((orbital_values, target_values), "grid", 0, 1)
    products = lax.dot_general(
        whole_slab, orbital_piece, (((1,), (1,)), ((), ())), preferred_element_type=jnp.float32
    )
    weighted = (potential * products).astype(jnp.bfloat16)
    group_total = jnp.dot(weighted, target_piece, preferred_element_type=jnp.float32)
    summed_rows = summed_on_arrival(group_total, IPTS, 0)
    return (-summed_rows).astype(jnp.bfloat16)


def solution(mesh):
    torus = Mesh(mesh.devices.reshape(mesh.shape["grid"], 2, 2), ("grid", "ipts_0", "ipts_1"))
    placed = (P(GRID_IPTS, None), P(GRID_IPTS, None), P(IPTS, "grid"), P("grid", IPTS))
    return jax.shard_map(
        local, mesh=torus, in_specs=placed, out_specs=P(GRID_IPTS, None), check_vma=False
    )
```

profile of v0, /device:TPU:1, one launch (start us, length us, event | category | flops | bytes accessed | tf_op | source)
XLA Modules:
  0.0 362.0 jit_solution(10757572754428285465)
XLA Ops:
  6.5 0.0 copy-start
  6.5 0.0 all-gather.7.cloned.1.call-start
  6.5 0.7 all-gather.7.cloned.1.call-update
  7.3 6.2 %all-gather.2 = s32[2,1,128]{2,1,0:T(1,128)S(1)} all-gather(s32[1,1,128]{2,1,0:T(1,128)} %bitcast.38), channel_id=2, replica_groups=mesh['grid'=32,'ipts_0'=2,'ipts_1'=2] {'ipts_0'}, dimensions={0}, use_global_device_ids=true | all-gather | bytes 1536 | tf_op jit(solution)/shard_map/all_gather | solution.py:20
  13.5 3.0 all-gather.3
  16.5 0.0 copy-done
  16.5 2.0 gather_fusion.1
  18.5 0.9 select_multiply_fusion
  19.4 5.1 %all-to-all-start = ((bf16[4,1,128,256]{3,2,1,0:T(8,128)(2,1)}), bf16[4,1,128,256]{3,2,1,0:T(8,128)(2,1)S(1)}, u32[]{:S(2)}, u32[]{:S(2)}) async-start(bf16[4,1,128,256]{3,2,1,0:T(8,128)(2,1)} %select_multiply_fusion), calls=%async_computation | async-start | bytes 524288 | tf_op jit(solution)/shard_map/all_to_all | solution.py:38
  24.5 0.0 all-gather.9.cloned.1.call-start
  24.5 0.7 fusion.8
  25.2 0.7 compare_and_fusion.1
  25.8 8.4 %all-to-all-done = bf16[4,1,128,256]{3,2,1,0:T(8,128)(2,1)S(1)} async-done(((bf16[4,1,128,256]{3,2,1,0:T(8,128)(2,1)}), bf16[4,1,128,256]{3,2,1,0:T(8,128)(2,1)S(1)}, u32[]{:S(2)}, u32[]{:S(2)}) %all-to-all-start) | async-done | bytes 262176 | tf_op jit(solution)/shard_map/all_to_all | solution.py:38
  34.3 19.9 %all-gather.7.cloned.1.call-done = bf16[2048,1024]{1,0:T(8,128)(2,1)} async-done(((bf16[512,1024]{1,0:T(8,128)(2,1)}), bf16[2048,1024]{1,0:T(8,128)(2,1)}) %all-gather.7.cloned.1.call-update) | async-done | bytes 4194320 | tf_op jit(solution)/shard_map/all_gather | solution.py:62
  54.2 3.8 %gather_fusion = bf16[128,1024]{1,0:T(8,128)(2,1)S(1)} fusion(bf16[2048,1024]{1,0:T(8,128)(2,1)} %all-gather.7.cloned.1.call-done, s32[1024]{0:T(1024)S(1)} %pad_clamp_fusion.1), kind=kCustom, calls=%fused_computation | custom fusion | bytes 524800 | tf_op jit(solution)/shard_map/jit(_take)/gather | solution.py:64
  57.9 0.1 broadcast_select_fusion
  58.0 0.8 pad_maximum_fusion
  58.8 0.0 all-gather.9.cloned.1.call-update
  58.8 22.6 %copy.8 = bf16[2048,4096]{0,1:T(8,128)(2,1)} copy(bf16[2048,4096]{1,0:T(8,128)(2,1)} %param.7) | data formatting | bytes 33554432 | tf_op args[3]
  81.4 207.0 %all-gather.9.cloned.1.call-done = bf16[4096,1280]{1,0:T(8,128)(2,1)} async-done(((bf16[128,1280]{1,0:T(8,128)(2,1)}), bf16[4096,1280]{1,0:T(8,128)(2,1)}) %all-gather.9.cloned.1.call-update) | async-done | bytes 10485776 | tf_op jit(solution)/shard_map/all_gather | solution.py:44
  288.4 34.1 %fusion.3 = f32[2048,256]{1,0:T(8,128)} fusion(bf16[2048,4096]{0,1:T(8,128)(2,1)} %copy.8, bf16[2048,1024]{1,0:T(8,128)(2,1)} %all-gather.7.cloned.1.call-done, bf16[4096,1280]{1,0:T(8,128)(2,1)} %all-gather.9.cloned.1.call-done), kind=kOutput, calls=%fused_computation.5 | convolution fusion | flops 21500002304 | bytes 33554432 | tf_op jit(solution)/shard_map/dot_general | solution.py:76
  322.5 31.8 %all_to_all.10 = f32[4,512,256]{2,1,0:T(8,128)S(1)} all-to-all(f32[4,512,256]{2,1,0:T(8,128)} %bitcast.32), channel_id=1, replica_groups=mesh['grid'=32,'ipts_0'=2,'ipts_1'=2] {'ipts_0','ipts_1'}, dimensions={0} | all-to-all | bytes 4194304 | tf_op jit(solution)/shard_map/all_to_all | solution.py:53
  354.3 0.2 reduce_sum.22
  354.4 0.7 negate_convert_fusion
  (9 shorter events, 0.1 us)
Async XLA Ops:
  6.5 10.0 %copy-start = (bf16[512,256]{1,0:T(8,128)(2,1)S(1)}, bf16[512,256]{1,0:T(8,128)(2,1)}, u32[]{:S(2)}) copy-start(bf16[512,256]{1,0:T(8,128)(2,1)} %param.5) | copy-start | bytes 786436
  6.5 47.6 %all-gather.7.cloned.1.call-start = ((), (), s32[]{:S(2)}) async-start(), calls=%async_computation.2 | async-start | bytes 5242880 | tf_op jit(solution)/shard_map/all_gather | solution.py:62
  19.4 14.8 %all-to-all-start = ((bf16[4,1,128,256]{3,2,1,0:T(8,128)(2,1)}), bf16[4,1,128,256]{3,2,1,0:T(8,128)(2,1)S(1)}, u32[]{:S(2)}, u32[]{:S(2)}) async-start(bf16[4,1,128,256]{3,2,1,0:T(8,128)(2,1)} %select_multiply_fusion), calls=%async_computation | async-start | bytes 524288 | tf_op jit(solution)/shard_map/all_to_all | solution.py:38
  24.5 263.9 %all-gather.9.cloned.1.call-start = ((), (), s32[]{:S(2)}) async-start(), calls=%async_computation.3 | async-start | bytes 10813440 | tf_op jit(solution)/shard_map/all_gather | solution.py:44
Sparse Core Ops, SparseCore 0:
  9.0 45.0 all-gather.6
  59.0 229.4 all-gather.8
where the time goes:
time: 363 us; the launch traced here: 362 us
  waiting for transfers between devices  236 us (65%)
  blocking collectives  41 us (11%)
  matrix products  34.1 us (9%)
  local copies, waits for them, and re-layouts  28.3 us (8%)
  between operations  13.5 us (4%)
  starting transfers between devices  5.07 us (1%)
  other arithmetic  4.09 us (1%)
    all_gather x1, waiting for transfers between devices, sent_together(): lax.all_gather(both, axis, axis=dim, tiled=True)  207 us
    dot_general x1, matrix products, local(): jnp.dot(weighted, target_piece, preferred_element_type=jnp.float32)  34.1 us
    all_to_all x1, blocking collectives, summed_on_arrival(): lax.all_to_all(split_up(value, dim, length), axis, 0, 0, tiled=True)  31.8 us
    unnamed x3, local copies, waits for them, and re-layouts  22.6 us
    all_gather x1, waiting for transfers between devices, local(): whole_slab = lax.all_gather(orbitals, IPTS, axis=0, tiled=True)  19.9 us
    all_gather x2, blocking collectives, gather_in_order(): pieces = lax.all_gather(pieces, axes[k])  9.21 us
    all_to_all x1, waiting for transfers between devices, sum_at_owner(): lax.all_to_all(pieces, axis, split_axis=0, concat_axis=0, tiled=True)  8.39 us
  transfers between devices with their start and end apart: 3, of which 3 were waited for; matrix products, arithmetic and copies ran while one was open for 7% of the time, Pallas kernels for 0%

commit v1 on v0

--- a/solution.py
+++ b/solution.py
@@ -55,11 +55,17 @@
 
 
 def local(orbitals, targets, points, potential):
+
+    def recast_rails(u_in):
+        vec_out = lax.all_to_all(jnp.stack([u_in] * lax.axis_size(IPTS)), IPTS, 0, 0)
+        y_new = jnp.concatenate(vec_out, 0)
+        return y_new
+
     groups = lax.axis_size(IPTS)
     own_rows = orbitals.shape[0]
     slab_length = own_rows * groups
     slab_start = lax.axis_index("grid") * slab_length
-    whole_slab = lax.all_gather(orbitals, IPTS, axis=0, tiled=True)
+    whole_slab = recast_rails(orbitals)
     every_group = whole_of(points, IPTS, (0, 1), 0)
     orbital_values = jnp.take(whole_slab, points[0] - slab_start, axis=0)
     offset = every_group - (slab_start + lax.axis_index(IPTS) * own_rows)

time: 363 us -> 398 us (1.096)
  waiting for transfers between devices: 236 us -> 257 us
  blocking collectives: 41 us -> 52.5 us
    all_to_all x1, waiting for transfers between devices: 8.39 us -> 48.8 us  [recast_rails(): lax.all_to_all(jnp.stack([u_in] * lax.axis_size(IPTS)), IPTS, 0, 0)]
    all_gather x1 -> x0, waiting for transfers between devices: 19.9 us -> none  [local(): whole_slab = lax.all_gather(orbitals, IPTS, axis=0, tiled=True)]
    all_to_all x0 -> x1, blocking collectives: none -> 11.4 us  [sum_at_owner(): lax.all_to_all(pieces, axis, split_axis=0, concat_axis=0, tiled=True)]
    unnamed x3 -> x5, local copies, waits for them, and re-layouts: 22.6 us -> 22.6 us
  transfers between devices with their start and end apart: 3 -> 2, of which waited for: 3 -> 2; matrix products, arithmetic and copies ran while one was open for 7% -> 6% of each run, Pallas kernels for 0% -> 0%
where the time goes in v1:
time: 398 us; the launch traced here: 397 us
  waiting for transfers between devices  257 us (65%)
  blocking collectives  52.5 us (13%)
  matrix products  34.1 us (9%)
  local copies, waits for them, and re-layouts  32 us (8%)
  between operations  13.5 us (3%)
  starting transfers between devices  5.84 us (1%)
    all_gather x1, waiting for transfers between devices, sent_together(): lax.all_gather(both, axis, axis=dim, tiled=True)  208 us
    all_to_all x1, waiting for transfers between devices, recast_rails(): lax.all_to_all(jnp.stack([u_in] * lax.axis_size(IPTS)), IPTS, 0, 0)  48.8 us
    dot_general x1, matrix products, local(): jnp.dot(weighted, target_piece, preferred_element_type=jnp.float32)  34.1 us
    all_to_all x1, blocking collectives, summed_on_arrival(): lax.all_to_all(split_up(value, dim, length), axis, 0, 0, tiled=True)  31.8 us
    unnamed x5, local copies, waits for them, and re-layouts  22.6 us
    all_to_all x1, blocking collectives, sum_at_owner(): lax.all_to_all(pieces, axis, split_axis=0, concat_axis=0, tiled=True)  11.4 us
    all_gather x2, blocking collectives, gather_in_order(): pieces = lax.all_gather(pieces, axes[k])  9.33 us
  transfers between devices with their start and end apart: 2, of which 2 were waited for; matrix products, arithmetic and copies ran while one was open for 6% of the time, Pallas kernels for 0%

profile of v1, /device:TPU:1, one launch (start us, length us, event | category | flops | bytes accessed | tf_op | source)
XLA Modules:
  0.0 396.6 jit_solution(5509853911635474851)
XLA Ops:
  6.5 0.0 copy-start
  6.5 0.0 copy-start.1
  6.5 6.3 %all-gather.2 = s32[2,1,128]{2,1,0:T(1,128)S(1)} all-gather(s32[1,1,128]{2,1,0:T(1,128)} %bitcast.39), channel_id=2, replica_groups=mesh['grid'=32,'ipts_0'=2,'ipts_1'=2] {'ipts_0'}, dimensions={0}, use_global_device_ids=true | all-gather | bytes 1536 | tf_op jit(solution)/shard_map/all_gather | solution.py:20
  12.9 3.0 all-gather.3
  15.9 0.0 copy-done
  16.0 2.0 gather_fusion.1
  17.9 0.2 select_multiply_fusion
  18.1 11.4 %all_to_all.15 = bf16[4,1,128,256]{3,2,1,0:T(8,128)(2,1)S(1)} all-to-all(bf16[4,1,128,256]{3,2,1,0:T(8,128)(2,1)S(1)} %select_multiply_fusion), channel_id=1, replica_groups=mesh['grid'=32,'ipts_0'=2,'ipts_1'=2] {'ipts_0','ipts_1'}, dimensions={0} | all-to-all | bytes 524288 | tf_op jit(solution)/shard_map/all_to_all | solution.py:38
  29.5 3.7 stack.2
  33.2 5.8 %all-to-all-start = ((bf16[4,512,1024]{2,1,0:T(8,128)(2,1)}), bf16[4,512,1024]{2,1,0:T(8,128)(2,1)}, u32[]{:S(2)}, u32[]{:S(2)}) async-start(bf16[4,512,1024]{2,1,0:T(8,128)(2,1)} %stack.2), calls=%async_computation | async-start | bytes 8388608 | tf_op jit(solution)/shard_map/all_to_all | solution.py:60
  39.0 0.0 all-gather.6.cloned.1.call-start
  39.0 0.0 copy-done.1
  39.1 48.8 %all-to-all-done = bf16[4,512,1024]{2,1,0:T(8,128)(2,1)} async-done(((bf16[4,512,1024]{2,1,0:T(8,128)(2,1)}), bf16[4,512,1024]{2,1,0:T(8,128)(2,1)}, u32[]{:S(2)}, u32[]{:S(2)}) %all-to-all-start) | async-done | bytes 4194336 | tf_op jit(solution)/shard_map/all_to_all | solution.py:60
  88.0 3.8 gather_fusion
  91.7 0.1 broadcast_select_fusion
  91.8 0.8 pad_maximum_fusion
  92.6 0.0 all-gather.6.cloned.1.call-update
  92.6 22.6 %copy.8 = bf16[2048,4096]{0,1:T(8,128)(2,1)} copy(bf16[2048,4096]{1,0:T(8,128)(2,1)} %param.7) | data formatting | bytes 33554432 | tf_op args[3]
  115.2 207.7 %all-gather.6.cloned.1.call-done = bf16[4096,1280]{1,0:T(8,128)(2,1)} async-done(((bf16[128,1280]{1,0:T(8,128)(2,1)}), bf16[4096,1280]{1,0:T(8,128)(2,1)}) %all-gather.6.cloned.1.call-update) | async-done | bytes 10485776 | tf_op jit(solution)/shard_map/all_gather | solution.py:44
  323.0 34.1 %fusion.3 = f32[2048,256]{1,0:T(8,128)} fusion(bf16[2048,4096]{0,1:T(8,128)(2,1)} %copy.8, bf16[2048,1024]{1,0:T(8,128)(2,1)} %bitcast.1, bf16[4096,1280]{1,0:T(8,128)(2,1)} %all-gather.6.cloned.1.call-done), kind=kOutput, calls=%fused_computation.5 | convolution fusion | flops 21500002304 | bytes 33554432 | tf_op jit(solution)/shard_map/dot_general | solution.py:82
  357.0 31.8 %all_to_all.16 = f32[4,512,256]{2,1,0:T(8,128)S(1)} all-to-all(f32[4,512,256]{2,1,0:T(8,128)} %bitcast.33), channel_id=1, replica_groups=mesh['grid'=32,'ipts_0'=2,'ipts_1'=2] {'ipts_0','ipts_1'}, dimensions={0} | all-to-all | bytes 4194304 | tf_op jit(solution)/shard_map/all_to_all | solution.py:53
  388.8 0.2 reduce_sum.22
  389.0 0.7 negate_convert_fusion
  (11 shorter events, 0.1 us)
Async XLA Ops:
  6.5 9.4 %copy-start = (bf16[512,256]{1,0:T(8,128)(2,1)S(1)}, bf16[512,256]{1,0:T(8,128)(2,1)}, u32[]{:S(2)}) copy-start(bf16[512,256]{1,0:T(8,128)(2,1)} %param.5) | copy-start | bytes 786436
  6.5 32.5 %copy-start.1 = (s32[1,128]{1,0:T(1,128)S(1)}, s32[1,128]{1,0:T(1,128)}, u32[]{:S(2)}) copy-start(s32[1,128]{1,0:T(1,128)} %param.6) | copy-start | bytes 1540
  33.2 54.8 %all-to-all-start = ((bf16[4,512,1024]{2,1,0:T(8,128)(2,1)}), bf16[4,512,1024]{2,1,0:T(8,128)(2,1)}, u32[]{:S(2)}, u32[]{:S(2)}) async-start(bf16[4,512,1024]{2,1,0:T(8,128)(2,1)} %stack.2), calls=%async_computation | async-start | bytes 8388608 | tf_op jit(solution)/shard_map/all_to_all | solution.py:60
  39.0 283.9 %all-gather.6.cloned.1.call-start = ((), (), s32[]{:S(2)}) async-start(), calls=%async_computation.3 | async-start | bytes 10813440 | tf_op jit(solution)/shard_map/all_gather | solution.py:44
Sparse Core Ops, SparseCore 0:
  92.7 230.1 all-gather.5
